TPU v7x, 32 devices: a whole 2x2x4 slice. The times are simulated.
32 devices in a mesh: expert: 16 (over z, y, x), replica: 2 (over core).
Axes of the slice: x: 2, y: 2, z: 4, core: 2. Of those that a mesh axis runs over, the one named last changes fastest.
Arguments:
- tokens: bfloat16 [1024, 7168], P('expert', 'replica'), may hold values from -6 to 6
- routes: int32 [1024, 8], P('expert'), may hold values from 0 to 15, all different within a row; in each aligned block of 64 rows (0 to 63, 64 to 127, ...) at most 64 rows name the same one
- route_scores: float32 [1024, 8], P('expert'), may hold values from 0.05 to 1
- placement: int32 [16], replicated, may hold values from 0 to 15, each once
- w_in: bfloat16 [16, 7168, 2, 1024], P('expert', 'replica'), may hold values from -0.0625 to 0.0625
- w_out: bfloat16 [16, 1024, 7168], P('expert', None, 'replica'), may hold values from -0.1875 to 0.1875
Outputs:
- mixed: bfloat16 [1024, 7168], P('expert', 'replica')
Inputs may be any that keep to these rules, and one draw needn't show every extreme that they name: `routes`: each row names 8 different logical experts. Among the 64 rows of each aligned block (the tokens of one index of the expert axis) no expert is named by more than 64 rows, a bound that some block reaches. `placement`: A permutation of the physical slots.
All inputs are finite; a program needn't handle non-finite values.
Results may differ from a plain program's by a relative error of at most 0.0057.
Values may be sent and summed in bfloat16 or wider, within the bound.
A program may use at most 128 MiB of HBM per device.

v0:
```python
import jax
import jax.numpy as jnp
from jax import lax
from jax.sharding import PartitionSpec as P


def on_device(tokens, routes, route_scores, placement, w_in, w_out):
    tok_rows, feature_cols = tokens.shape
    route_count = routes.shape[1]
    experts = placement.shape[0]
    hidden_units = w_in.shape[3]
    capacity = min(tok_rows, max(2, 2 * tok_rows * route_count // experts))
    slot_total = experts * capacity
    expert_ids = jnp.arange(experts, dtype=jnp.int32)
    route_table = routes[:, :, None] == expert_ids
    physical = jnp.sum(jnp.where(route_table, placement, 0), axis=-1)
    flat_slots = physical.reshape(-1)
    onehot = (flat_slots[:, None] == expert_ids).astype(jnp.int32)
    earlier = jnp.sum((jnp.cumsum(onehot, axis=0) - onehot) * onehot, axis=1)
    position = (flat_slots * capacity + earlier).reshape(tok_rows, route_count)
    slot_index = jnp.arange(slot_total, dtype=jnp.int32)
    placing = jnp.any(position[None, :, :] == slot_index[:, None, None], axis=-1).astype(
        jnp.bfloat16
    )
    outgoing = jnp.dot(placing, tokens, preferred_element_type=jnp.float32).astype(jnp.bfloat16)
    incoming = lax.all_to_all(outgoing, "expert", split_axis=0, concat_axis=0, tiled=True)
    weights_in = w_in[0].reshape(feature_cols, 2 * hidden_units)
    weights_out = w_out[0]
    partial_value = jnp.dot(incoming, weights_in, preferred_element_type=jnp.float32)
    partial_value = partial_value.reshape(slot_total, 2, hidden_units)
    shares = lax.psum_scatter(partial_value, "replica", scatter_dimension=2, tiled=True)
    active = (jax.nn.silu(shares[:, 0]) * shares[:, 1]).astype(jnp.bfloat16)
    result = jnp.dot(
        lax.all_gather(active, "replica", axis=1, tiled=True),
        weights_out,
        preferred_element_type=jnp.float32,
    )
    expert_out = result.astype(jnp.bfloat16)
    returned = lax.all_to_all(expert_out, "expert", split_axis=0, concat_axis=0, tiled=True)
    route_weight = 2.5 * route_scores / jnp.sum(route_scores, axis=1, keepdims=True)
    picked = returned[position.reshape(-1)].reshape(tok_rows, route_count, feature_cols)
    mixed = jnp.sum(picked.astype(jnp.float32) * route_weight[:, :, None], axis=1)
    return mixed.astype(jnp.bfloat16)


def solution(mesh):
    in_specs = (
        P("expert", "replica"),
        P("expert", None),
        P("expert", None),
        P(),
        P("expert", "replica", None, None),
        P("expert", None, "replica"),
    )
    out_specs = P("expert", "replica")
    return jax.shard_map(
        on_device, mesh=mesh, in_specs=in_specs, out_specs=out_specs, check_vma=False
    )
```

profile of v0, /device:TPU:28, one launch (start us, length us, event | category | flops | bytes accessed | tf_op | source)
XLA Modules:
  0.0 454.1 jit_solution(2317390866444530714)
XLA Ops:
  6.5 0.8 select_reduce_fusion
  7.4 0.1 copy.14
  7.5 0.1 eq.58
  7.6 0.1 eq.54
  7.7 1.2 reduce-window.6
  8.8 0.2 slice_reduce_fusion
  9.1 0.1 fusion.7
  9.2 0.1 reduce_sum.42
  9.3 0.1 copy.17
  9.3 0.1 copy.18
  9.4 0.7 fusion.4
  10.2 5.1 %convolution_convert_fusion.1 = bf16[1024,3584]{1,0:T(8,128)(2,1)} fusion(pred[1024,64]{0,1:T(8,128)(4,1)S(1)} %fusion.4, bf16[64,3584]{1,0:T(8,128)(2,1)S(1)} %copy-done), kind=kOutput, calls=%fused_computation.2 | convolution fusion | flops 473432064 | bytes 7864320 | tf_op jit(solution)/shard_map/dot_general | solution.py:25
  15.3 7.0 %all-to-all-start = ((bf16[16,64,3584]{2,1,0:T(8,128)(2,1)}), bf16[16,64,3584]{2,1,0:T(8,128)(2,1)}, u32[]{:S(2)}, u32[]{:S(2)}) async-start(bf16[16,64,3584]{2,1,0:T(8,128)(2,1)} %bitcast.55), calls=%async_computation | async-start | bytes 14680064 | tf_op jit(solution)/shard_map/all_to_all | solution.py:26
  22.2 0.0 reduce-scatter.2.cloned.1.call-start
  22.3 16.0 %copy.23 = bf16[448,8,2,1024]{3,1,2,0:T(8,128)(2,1)} copy(bf16[448,8,2,1024]{3,2,1,0:T(2,128)(2,1)} %bitcast.56) | data formatting | bytes 29360128
  38.3 18.8 %copy.19 = bf16[2048,3584]{1,0:T(8,128)(2,1)} copy(bf16[2048,3584]{0,1:T(8,128)(2,1)} %bitcast.54) | data formatting | bytes 29360128 | tf_op jit(solution)/shard_map/dot_general | solution.py:29
  57.1 131.5 %all-to-all-done = bf16[16,64,3584]{2,1,0:T(8,128)(2,1)} async-done(((bf16[16,64,3584]{2,1,0:T(8,128)(2,1)}), bf16[16,64,3584]{2,1,0:T(8,128)(2,1)}, u32[]{:S(2)}, u32[]{:S(2)}) %all-to-all-start) | async-done | bytes 7340064 | tf_op jit(solution)/shard_map/all_to_all | solution.py:26
  188.6 21.6 %fusion.10 = f32[1024,2,1024]{2,0,1:T(8,128)} fusion(bf16[1024,3584,1]{1,0,2:T(8,128)(2,1)} %bitcast.3, bf16[2,1024,3584]{2,1,0:T(8,128)(2,1)} %bitcast.57), kind=kOutput, calls=%fused_computation.28 | convolution fusion | flops 15032385536 | bytes 30408704 | tf_op jit(solution)/shard_map/dot_general | solution.py:29
  210.2 0.0 reduce-scatter.2.cloned.1.call-update
  210.2 0.0 all-gather.2.cloned.1.call-start
  210.2 16.7 %reduce-scatter.2.cloned.1.call-done = f32[1024,2,512]{2,0,1:T(8,128)} async-done(((f32[1024,2,1024]{2,0,1:T(8,128)}), f32[1024,2,512]{2,0,1:T(8,128)}) %reduce-scatter.2.cloned.1.call-update) | async-done | bytes 4194320 | tf_op jit(solution)/shard_map/reduce_scatter | solution.py:31
  226.9 3.8 fusion.3
  230.8 0.0 all-gather.2.cloned.1.call-update
  230.8 11.9 %all-gather.2.cloned.1.call-done = bf16[1024,1024]{1,0:T(8,128)(2,1)} async-done(((bf16[1024,512]{1,0:T(8,128)(2,1)}), bf16[1024,1024]{1,0:T(8,128)(2,1)}) %all-gather.2.cloned.1.call-update) | async-done | bytes 2097168 | tf_op jit(solution)/shard_map/all_gather | solution.py:34
  242.7 12.5 %convolution_convert_fusion = bf16[1024,3584]{1,0:T(8,128)(2,1)} fusion(bf16[1024,1024]{1,0:T(8,128)(2,1)} %all-gather.2.cloned.1.call-done, bf16[1,1024,3584]{2,1,0:T(8,128)(2,1)} %param.11), kind=kOutput, calls=%fused_computation.1 | convolution fusion | flops 7519862784 | bytes 16777216 | tf_op jit(solution)/shard_map/dot_general | solution.py:33
  255.2 7.1 %all-to-all-start.1 = ((bf16[16,64,3584]{2,1,0:T(8,128)(2,1)}), bf16[16,64,3584]{2,1,0:T(8,128)(2,1)}, u32[]{:S(2)}, u32[]{:S(2)}) async-start(bf16[16,64,3584]{2,1,0:T(8,128)(2,1)} %bitcast.58), calls=%async_computation.2 | async-start | bytes 14680064 | tf_op jit(solution)/shard_map/all_to_all | solution.py:39
  262.3 0.1 copy.20
  262.4 0.1 mul.49
  262.5 0.1 copy.21
  262.6 166.8 %all-to-all-done.1 = bf16[16,64,3584]{2,1,0:T(8,128)(2,1)} async-done(((bf16[16,64,3584]{2,1,0:T(8,128)(2,1)}), bf16[16,64,3584]{2,1,0:T(8,128)(2,1)}, u32[]{:S(2)}, u32[]{:S(2)}) %all-to-all-start.1) | async-done | bytes 7340064 | tf_op jit(solution)/shard_map/all_to_all | solution.py:39
  429.4 12.0 %gather_fusion = bf16[512,3584]{1,0:T(8,128)(2,1)} fusion(bf16[1024,3584]{1,0:T(8,128)(2,1)} %bitcast.10, s32[1024]{0:T(1024)S(1)} %pad_clamp_fusion), kind=kCustom, calls=%fused_computation | custom fusion | bytes 7342080 | tf_op jit(solution)/shard_map/gather | solution.py:41
  441.4 5.8 %fusion = bf16[64,3584]{1,0:T(8,128)(2,1)} fusion(bf16[512,3584]{1,0:T(8,128)(2,1)} %gather_fusion, f32[64,8]{1,0:T(8,128)S(1)} %copy.21), kind=kLoop, calls=%fused_computation.4 | loop fusion | flops 5275648 | bytes 4130816 | tf_op jit(solution)/shard_map/reduce_sum | solution.py:42
  (14 shorter events, 0.1 us)
Async XLA Ops:
  6.5 3.6 copy-start
  15.3 173.3 %all-to-all-start = ((bf16[16,64,3584]{2,1,0:T(8,128)(2,1)}), bf16[16,64,3584]{2,1,0:T(8,128)(2,1)}, u32[]{:S(2)}, u32[]{:S(2)}) async-start(bf16[16,64,3584]{2,1,0:T(8,128)(2,1)} %bitcast.55), calls=%async_computation | async-start | bytes 14680064 | tf_op jit(solution)/shard_map/all_to_all | solution.py:26
  22.2 204.7 %reduce-scatter.2.cloned.1.call-start = ((), (), s32[]{:S(2)}) async-start(), calls=%async_computation.3 | async-start | bytes 12582912 | tf_op jit(solution)/shard_map/reduce_scatter | solution.py:31
  210.2 32.5 %all-gather.2.cloned.1.call-start = ((), (), s32[]{:S(2)}) async-start(), calls=%async_computation.4 | async-start | bytes 3145728 | tf_op jit(solution)/shard_map/all_gather | solution.py:34
  255.2 7.2 %copy-start.2 = (f32[64,8]{0,1:T(8,128)S(1)}, f32[64,8]{0,1:T(8,128)}, u32[]{:S(2)}) copy-start(f32[64,8]{0,1:T(8,128)} %param.8) | copy-start | bytes 6148
  255.2 174.2 %all-to-all-start.1 = ((bf16[16,64,3584]{2,1,0:T(8,128)(2,1)}), bf16[16,64,3584]{2,1,0:T(8,128)(2,1)}, u32[]{:S(2)}, u32[]{:S(2)}) async-start(bf16[16,64,3584]{2,1,0:T(8,128)(2,1)} %bitcast.58), calls=%async_computation.2 | async-start | bytes 14680064 | tf_op jit(solution)/shard_map/all_to_all | solution.py:39
  429.4 17.8 %copy-start.1 = (bf16[64,3584]{1,0:T(8,128)(2,1)S(1)}, bf16[64,3584]{1,0:T(8,128)(2,1)}, u32[]{:S(2)}) copy-start(bf16[64,3584]{1,0:T(8,128)(2,1)} %param.6) | copy-start | bytes 1376260
Sparse Core Ops, SparseCore 0:
  210.3 16.5 reduce-scatter.1
  230.9 11.7 all-gather.1
where the time goes:
time: 455 us; the launch traced here: 454 us
  waiting for transfers between devices  327 us (72%)
  local copies, waits for them, and re-layouts  47.8 us (11%)
  matrix products  39.3 us (9%)
  starting transfers between devices  14.1 us (3%)
  between operations  13.5 us (3%)
  other arithmetic  12.6 us (3%)
    all_to_all x1, waiting for transfers between devices, on_device(): lax.all_to_all(expert_out, 'expert', split_axis=0, concat_axis=0, tiled=T...  167 us
    all_to_all x1, waiting for transfers between devices, on_device(): lax.all_to_all(outgoing, 'expert', split_axis=0, concat_axis=0, tiled=True)  131 us
    dot_general x1, matrix products, on_device(): jnp.dot(incoming, weights_in, preferred_element_type=jnp.float32)  21.6 us
    dot_general x1, local copies, waits for them, and re-layouts, on_device(): jnp.dot(incoming, weights_in, preferred_element_type=jnp.float32)  18.8 us
    reduce_scatter x1, waiting for transfers between devices, on_device(): lax.psum_scatter(partial_value, 'replica', scatter_dimension=2, tiled=True)  16.7 us
    unnamed x7, local copies, waits for them, and re-layouts  16 us
    dot_general x1, matrix products, on_device(): jnp.dot(lax.all_gather(active, 'replica', axis=1, tiled=True), weights_ou...  12.5 us
    gather x1, local copies, waits for them, and re-layouts, on_device(): returned[position.reshape(-1)].reshape(tok_rows, route_count, feature_cols)  12 us
  transfers between devices with their start and end apart: 4, of which 4 were waited for; matrix products, arithmetic and copies ran while one was open for 8% of the time, Pallas kernels for 0%

commit v1 on v0

--- a/solution.py
+++ b/solution.py
@@ -4,7 +4,7 @@
 from jax.sharding import PartitionSpec as P
 
 
-def on_device(tokens, routes, route_scores, placement, w_in, w_out):
+def packed(tokens, routes, route_scores, placement, w_in, w_out):
     tok_rows, feature_cols = tokens.shape
     route_count = routes.shape[1]
     experts = placement.shape[0]
@@ -43,6 +43,44 @@
     return mixed.astype(jnp.bfloat16)
 
 
+def expert_weights(routes, route_scores, placement):
+    experts = placement.shape[0]
+    expert_ids = jnp.arange(experts, dtype=jnp.int32)
+    physical = jnp.sum(jnp.where(routes[:, :, None] == expert_ids, placement, 0), axis=-1)
+    route_weight = 2.5 * route_scores / jnp.sum(route_scores, axis=1, keepdims=True)
+    return jnp.sum(
+        jnp.where(physical[:, :, None] == expert_ids, route_weight[:, :, None], 0.0), axis=1
+    )
+
+
+def dense(tokens, routes, route_scores, placement, w_in, w_out):
+    feature_cols = tokens.shape[1]
+    hidden_units = w_in.shape[3]
+    table = expert_weights(routes, route_scores, placement)
+    mine = lax.all_to_all(table, "expert", split_axis=1, concat_axis=0, tiled=True)
+    incoming = lax.all_gather(tokens, "expert", axis=0, tiled=True)
+    rows = incoming.shape[0]
+    weights_in = w_in[0].reshape(feature_cols, 2 * hidden_units)
+    partial_value = jnp.dot(incoming, weights_in, preferred_element_type=jnp.float32)
+    partial_value = partial_value.reshape(rows, 2, hidden_units)
+    shares = lax.psum_scatter(partial_value, "replica", scatter_dimension=2, tiled=True)
+    active = (jax.nn.silu(shares[:, 0]) * shares[:, 1]).astype(jnp.bfloat16)
+    result = jnp.dot(
+        lax.all_gather(active, "replica", axis=1, tiled=True),
+        w_out[0],
+        preferred_element_type=jnp.float32,
+    )
+    weighted = (result.astype(jnp.bfloat16).astype(jnp.float32) * mine).astype(jnp.bfloat16)
+    return lax.psum_scatter(weighted, "expert", scatter_dimension=0, tiled=True)
+
+
+def on_device(tokens, routes, route_scores, placement, w_in, w_out):
+    tok_rows = tokens.shape[0]
+    if 2 * tok_rows * routes.shape[1] // placement.shape[0] >= tok_rows:
+        return dense(tokens, routes, route_scores, placement, w_in, w_out)
+    return packed(tokens, routes, route_scores, placement, w_in, w_out)
+
+
 def solution(mesh):
     in_specs = (
         P("expert", "replica"),

time: 455 us -> 347 us (0.76)
  the two profiles are of different devices: /device:TPU:28 before, /device:TPU:0 now
where the time goes in v1:
time: 347 us; the launch traced here: 345 us
  waiting for transfers between devices  245 us (71%)
  local copies, waits for them, and re-layouts  34.9 us (10%)
  matrix products  34.1 us (10%)
  blocking collectives  14 us (4%)
  between operations  13.2 us (4%)
  other arithmetic  3.98 us (1%)
    reduce_scatter x1, waiting for transfers between devices, dense(): return lax.psum_scatter(weighted, 'expert', scatter_dimension=0, tiled=True)  156 us
    all_gather x1, waiting for transfers between devices, dense(): incoming = lax.all_gather(tokens, 'expert', axis=0, tiled=True)  73.5 us
    dot_general x1, matrix products, dense(): jnp.dot(incoming, weights_in, preferred_element_type=jnp.float32)  21.6 us
    dot_general x1, local copies, waits for them, and re-layouts, dense(): jnp.dot(incoming, weights_in, preferred_element_type=jnp.float32)  18.8 us
    unnamed x7, local copies, waits for them, and re-layouts  16.1 us
    reduce_scatter x1, waiting for transfers between devices, dense(): lax.psum_scatter(partial_value, 'replica', scatter_dimension=2, tiled=True)  14.7 us
    all_to_all x1, blocking collectives, dense(): lax.all_to_all(table, 'expert', split_axis=1, concat_axis=0, tiled=True)  14 us
    dot_general x1, matrix products, dense(): jnp.dot(lax.all_gather(active, 'replica', axis=1, tiled=True), w_out[0],...  12.5 us
  transfers between devices with their start and end apart: 4, of which 3 were waited for; matrix products, arithmetic and copies ran while one was open for 10% of the time, Pallas kernels for 0%

profile of v1, /device:TPU:0, one launch (start us, length us, event | category | flops | bytes accessed | tf_op | source)
XLA Modules:
  0.0 345.0 jit_solution(17655661760736529164)
XLA Ops:
  6.5 0.0 all-gather.3.cloned.1.call-start
  6.5 0.7 all-gather.3.cloned.1.call-update
  7.3 0.0 reduce-scatter.3.cloned.1.call-start
  7.3 16.0 %copy.18 = bf16[448,8,2,1024]{3,1,2,0:T(8,128)(2,1)} copy(bf16[448,8,2,1024]{3,2,1,0:T(2,128)(2,1)} %bitcast.32) | data formatting | bytes 29360128
  23.3 18.8 %copy.16 = bf16[2048,3584]{1,0:T(8,128)(2,1)} copy(bf16[2048,3584]{0,1:T(8,128)(2,1)} %bitcast.31) | data formatting | bytes 29360128 | tf_op jit(solution)/shard_map/dot_general | solution.py:64
  42.1 73.5 %all-gather.3.cloned.1.call-done = bf16[1024,3584]{1,0:T(8,128)(2,1)} async-done(((bf16[64,3584]{1,0:T(8,128)(2,1)}), bf16[1024,3584]{1,0:T(8,128)(2,1)}) %all-gather.3.cloned.1.call-update) | async-done | bytes 7340048 | tf_op jit(solution)/shard_map/all_gather | solution.py:61
  115.6 21.6 %fusion.3 = f32[1024,2,1024]{2,0,1:T(8,128)} fusion(bf16[2,1024,3584]{2,1,0:T(8,128)(2,1)} %bitcast.33, bf16[1024,3584]{1,0:T(8,128)(2,1)} %all-gather.3.cloned.1.call-done), kind=kOutput, calls=%fused_computation.3 | convolution fusion | flops 15032385536 | bytes 30408704 | tf_op jit(solution)/shard_map/dot_general | solution.py:64
  137.2 0.0 copy-start
  137.2 0.0 copy-start.1
  137.2 0.0 copy-start.2
  137.2 0.0 reduce-scatter.3.cloned.1.call-update
  137.2 0.0 all-gather.5.cloned.1.call-start
  137.3 14.7 %reduce-scatter.3.cloned.1.call-done = f32[1024,2,512]{2,0,1:T(8,128)} async-done(((f32[1024,2,1024]{2,0,1:T(8,128)}), f32[1024,2,512]{2,0,1:T(8,128)}) %reduce-scatter.3.cloned.1.call-update) | async-done | bytes 4194320 | tf_op jit(solution)/shard_map/reduce_scatter | solution.py:66
  151.9 3.8 %fusion.6 = bf16[1024,512]{1,0:T(8,128)(2,1)} fusion(f32[1024,2,512]{2,0,1:T(8,128)} %reduce-scatter.3.cloned.1.call-done), kind=kLoop, calls=%fused_computation.7 | loop fusion | flops 3145728 | bytes 5242880 | tf_op jit(solution)/shard_map/convert_element_type | solution.py:67
  155.8 0.0 all-gather.5.cloned.1.call-update
  155.8 0.0 reduce-scatter.5.cloned.1.call-start
  155.8 0.0 copy-done
  155.9 0.0 copy-done.1
  155.9 0.0 copy-done.2
  155.9 0.1 select_reduce_fusion.1
  156.0 14.0 %all_to_all.16 = f32[64,16,1]{0,2,1:T(1,128)S(1)} all-to-all(f32[64,16,1]{0,2,1:T(1,128)S(1)} %bitcast.34), channel_id=1, replica_groups=mesh['expert'=16,'replica'=2] {'expert'}, dimensions={1} | all-to-all | bytes 8192 | tf_op jit(solution)/shard_map/all_to_all | solution.py:60
  170.1 0.1 mul.27
  170.1 0.0 all-gather.5.cloned.1.call-done
  170.1 12.5 %multiply_convert_fusion = bf16[1024,3584]{1,0:T(8,128)(2,1)} fusion(bf16[1024,1024]{1,0:T(8,128)(2,1)} %all-gather.5.cloned.1.call-done, bf16[1,1024,3584]{2,1,0:T(8,128)(2,1)} %param.11, f32[1024]{0:T(1024)S(1)} %mul.27), kind=kOutput, calls=%fused_computation | convolution fusion | flops 7530872832 | bytes 16781312 | tf_op jit(solution)/shard_map/dot_general | solution.py:68
  182.6 0.0 reduce-scatter.5.cloned.1.call-update
  182.7 155.8 %reduce-scatter.5.cloned.1.call-done = bf16[64,3584]{1,0:T(8,128)(2,1)} async-done(((bf16[1024,3584]{1,0:T(8,128)(2,1)}), bf16[64,3584]{1,0:T(8,128)(2,1)}) %reduce-scatter.5.cloned.1.call-update) | async-done | bytes 458768 | tf_op jit(solution)/shard_map/reduce_scatter | solution.py:74
  (4 shorter events, 0.1 us)
Async XLA Ops:
  6.5 109.1 %all-gather.3.cloned.1.call-start = ((), (), s32[]{:S(2)}) async-start(), calls=%async_computation.3 | async-start | bytes 7798784 | tf_op jit(solution)/shard_map/all_gather | solution.py:61
  7.3 144.7 %reduce-scatter.3.cloned.1.call-start = ((), (), s32[]{:S(2)}) async-start(), calls=%async_computation.4 | async-start | bytes 12582912 | tf_op jit(solution)/shard_map/reduce_scatter | solution.py:66
  137.2 18.7 %copy-start = (f32[64,8]{0,1:T(8,128)S(1)}, f32[64,8]{0,1:T(8,128)}, u32[]{:S(2)}) copy-start(f32[64,8]{0,1:T(8,128)} %param.8) | copy-start | bytes 6148
  137.2 18.7 %copy-start.1 = (s32[64,8]{0,1:T(8,128)S(1)}, s32[64,8]{0,1:T(8,128)}, u32[]{:S(2)}) copy-start(s32[64,8]{0,1:T(8,128)} %param.7) | copy-start | bytes 6148
  137.2 18.7 %copy-start.2 = (s32[16]{0:T(128)S(1)}, s32[16]{0:T(128)}, u32[]{:S(2)}) copy-start(s32[16]{0:T(128)} %param.9) | copy-start | bytes 196
  137.2 32.9 %all-gather.5.cloned.1.call-start = ((), (), s32[]{:S(2)}) async-start(), calls=%async_computation.5 | async-start | bytes 3145728 | tf_op jit(solution)/shard_map/all_gather | solution.py:69
  155.8 182.7 %reduce-scatter.5.cloned.1.call-start = ((), (), s32[]{:S(2)}) async-start(), calls=%async_computation.6 | async-start | bytes 7798784 | tf_op jit(solution)/shard_map/reduce_scatter | solution.py:74
Sparse Core Ops, SparseCore 0:
  10.0 105.5 all-gather.2
  137.3 14.5 reduce-scatter.2
  155.9 11.8 all-gather.4
  182.8 155.6 reduce-scatter.4

commit v2 on v0

--- a/solution.py
+++ b/solution.py
@@ -1,10 +1,17 @@
 import jax
 import jax.numpy as jnp
 from jax import lax
+from jax.experimental import pallas as pl
+from jax.experimental.pallas import tpu as pltpu
 from jax.sharding import PartitionSpec as P
 
-
-def on_device(tokens, routes, route_scores, placement, w_in, w_out):
+LANES = 128
+TILE = 256
+MESH = pl.DeviceIdType.MESH
+LINE = 4
+
+
+def packed(tokens, routes, route_scores, placement, w_in, w_out):
     tok_rows, feature_cols = tokens.shape
     route_count = routes.shape[1]
     experts = placement.shape[0]
@@ -43,6 +50,285 @@
     return mixed.astype(jnp.bfloat16)
 
 
+def expert_weights(routes, route_scores, placement):
+    experts = placement.shape[0]
+    expert_ids = jnp.arange(experts, dtype=jnp.int32)
+    physical = jnp.sum(jnp.where(routes[:, :, None] == expert_ids, placement, 0), axis=-1)
+    route_weight = 2.5 * route_scores / jnp.sum(route_scores, axis=1, keepdims=True)
+    return jnp.sum(
+        jnp.where(physical[:, :, None] == expert_ids, route_weight[:, :, None], 0.0), axis=1
+    )
+
+
+def layer_kernel(
+    ext_ref, w_in_ref, w_out_ref, out_ref,
+    xs, wg, wu, stage, wo, contrib, from_b, from_a, from_z, part, sent, got, act,
+    w_sem, wo_sem, z_send, a_send, b_send, x_recv,
+    p_send, p_recv, rb_send, rb_recv, ra_send, ra_recv, rz_send, rz_recv,
+):
+    rows, width = ext_ref.shape
+    cols = out_ref.shape[1]
+    hidden = wg.shape[1]
+    tiles = hidden // TILE
+    me = lax.axis_index("expert")
+    core = lax.axis_index("replica")
+    x, y, z = me % 2, (me // 2) % 2, me // 4
+    flip_x, flip_y = me + 1 - 2 * x, me + 2 - 4 * y
+    near_a = (1 - core) * flip_x + core * flip_y
+    near_b = (1 - core) * flip_y + core * flip_x
+    base = me - 4 * z
+
+    def line(d):
+        return (z + d) % LINE
+
+    barrier = pltpu.get_barrier_semaphore()
+    peers = [(near_a, core), (near_b, core), (me, 1 - core)]
+    peers += [(base + 4 * line(d), core) for d in range(1, LINE)]
+    for peer in peers:
+        pl.semaphore_signal(barrier, inc=1, device_id=peer, device_id_type=MESH)
+    pl.semaphore_wait(barrier, len(peers))
+
+    def remote(src, dst, send, recv, chip, on_core=None):
+        return pltpu.make_async_remote_copy(
+            src_ref=src, dst_ref=dst, send_sem=send, recv_sem=recv,
+            device_id=(chip, core if on_core is None else on_core), device_id_type=MESH,
+        )
+
+    def arrived(ref, recv):
+        remote(ref, ref, a_send.at[0], recv, near_a).wait_recv()
+
+    def stage_copy(ct):
+        return pltpu.make_async_copy(
+            w_in_ref.at[0, :, :, pl.ds(ct * LANES, LANES)], stage.at[ct % 2], w_sem.at[ct % 2]
+        )
+
+    pending = []
+
+    def go(copy):
+        copy.start()
+        pending.append(copy)
+
+    go(remote(ext_ref, xs.at[LINE + z], a_send.at[0], x_recv.at[LINE + z], near_a))
+    go(remote(ext_ref, xs.at[2 * LINE + z], b_send.at[0], x_recv.at[2 * LINE + z], near_b))
+    for d in (1, 3, 2):
+        go(remote(ext_ref, xs.at[z], z_send.at[d - 1], x_recv.at[z], base + 4 * line(d)))
+    stage_copy(0).start()
+    stage_copy(1).start()
+    out_weights = pltpu.make_async_copy(w_out_ref.at[0], wo, wo_sem)
+    out_weights.start()
+    xs[z] = ext_ref[...]
+
+    row = lax.broadcasted_iota(jnp.int32, (TILE, TILE), 0)
+    col = lax.broadcasted_iota(jnp.int32, (TILE, TILE), 1)
+    half = TILE // 2
+    wanted = jnp.where(row < half, 2 * row, 2 * (row - half) + 1)
+    sorter = (col == wanted).astype(jnp.float32).astype(jnp.bfloat16)
+
+    def sort_tile(ct):
+        stage_copy(ct).wait()
+        flat = stage.at[ct % 2].reshape(2 * cols, LANES)
+
+        def body(k, carry):
+            piece = flat[pl.ds(pl.multiple_of(k * TILE, TILE), TILE), :]
+            both = jnp.dot(sorter, piece, preferred_element_type=jnp.float32).astype(jnp.bfloat16)
+            at = pl.ds(pl.multiple_of(k * half, half), half)
+            wg[at, ct * LANES:(ct + 1) * LANES] = both[:half]
+            wu[at, ct * LANES:(ct + 1) * LANES] = both[half:]
+            return carry
+
+        lax.fori_loop(0, 2 * cols // TILE, body, 0)
+        if ct + 2 < hidden // LANES:
+            stage_copy(ct + 2).start()
+
+    def own_line_on(d, n):
+        slot = line(d)
+        arrived(xs.at[slot], x_recv.at[slot])
+        go(remote(xs.at[slot], xs.at[LINE + slot], a_send.at[n], x_recv.at[LINE + slot], near_a))
+        to = 2 * LINE + slot
+        go(remote(xs.at[slot], xs.at[to], b_send.at[n], x_recv.at[to], near_b))
+
+    def a_line_on(d, n):
+        slot = LINE + line(d)
+        arrived(xs.at[slot], x_recv.at[slot])
+        to = 2 * LINE + slot
+        go(remote(xs.at[slot], xs.at[to], b_send.at[LINE + n], x_recv.at[to], near_b))
+
+    all_tiles = list(range(hidden // LANES))
+    quarter = max(1, len(all_tiles) // 4)
+    for ct in all_tiles[:2 * quarter]:
+        sort_tile(ct)
+    own_line_on(1, 1)
+    a_line_on(0, 0)
+    for ct in all_tiles[2 * quarter:3 * quarter]:
+        sort_tile(ct)
+    own_line_on(3, 2)
+    a_line_on(1, 1)
+    for ct in all_tiles[3 * quarter:]:
+        sort_tile(ct)
+    own_line_on(2, 3)
+    a_line_on(3, 2)
+    a_line_on(2, 3)
+    out_weights.wait()
+
+    lane = lax.broadcasted_iota(jnp.int32, (LINE * rows, LANES), 1)
+    mine = (lane % 16 == me) & (lane < 48)
+
+    def exchange(s, j):
+        return remote(sent.at[s, j], got.at[s, j], p_send.at[s, j], p_recv.at[s, j], me, 1 - core)
+
+    def step(s, group):
+        block = pl.ds(group * LINE, LINE)
+
+        def first(j, carry):
+            at = pl.ds(pl.multiple_of(j * TILE, TILE), TILE)
+            value = xs[block, :, :cols].reshape(LINE * rows, cols)
+            gate = jnp.dot(value, wg[:, at], preferred_element_type=jnp.float32)
+            up = jnp.dot(value, wu[:, at], preferred_element_type=jnp.float32)
+            part[j, 0] = gate
+            part[j, 1] = up
+            sent[s, j, 0] = gate.astype(jnp.bfloat16)
+            sent[s, j, 1] = up.astype(jnp.bfloat16)
+            exchange(s, j).start()
+            return carry
+
+        lax.fori_loop(0, tiles, first, 0)
+
+        def second(j, carry):
+            exchange(s, j).wait_recv()
+            gate = part[j, 0] + got[s, j, 0].astype(jnp.float32)
+            up = part[j, 1] + got[s, j, 1].astype(jnp.float32)
+            act[:, pl.ds(pl.multiple_of(j * TILE, TILE), TILE)] = (
+                gate / (1.0 + jnp.exp(-gate)) * up
+            ).astype(jnp.bfloat16)
+            return carry
+
+        lax.fori_loop(0, tiles, second, 0)
+        scales = xs[block, :, cols:].reshape(LINE * rows, LANES).astype(jnp.float32)
+        scale = jnp.sum(jnp.where(mine, scales, 0.0), axis=1, keepdims=True)
+
+        def third(j, carry):
+            at = pl.ds(pl.multiple_of(j * TILE, TILE), TILE)
+            value = jnp.dot(act[...], wo[:, at], preferred_element_type=jnp.float32)
+            value = value.astype(jnp.bfloat16).astype(jnp.float32) * scale
+            contrib[block, :, at] = value.astype(jnp.bfloat16).reshape(LINE, rows, TILE)
+            return carry
+
+        lax.fori_loop(0, cols // TILE, third, 0)
+
+    step(0, 0)
+    for d in range(LINE):
+        slot = 2 * LINE + line(d)
+        arrived(xs.at[slot], x_recv.at[slot])
+    step(1, 1 + core)
+    step(2, 2 - core)
+    order = (1, 3, 2, 0)
+    for n, d in enumerate(order):
+        src = 2 * LINE + line(d)
+        to = line(d)
+        go(remote(contrib.at[src], from_b.at[to], rb_send.at[n], rb_recv.at[to], near_b))
+    for d in range(LINE):
+        slot = 3 * LINE + line(d)
+        arrived(xs.at[slot], x_recv.at[slot])
+    step(3, 3)
+    for n, d in enumerate(order):
+        src = 3 * LINE + line(d)
+        to = LINE + line(d)
+        go(remote(contrib.at[src], from_b.at[to], rb_send.at[LINE + n], rb_recv.at[to], near_b))
+
+    def plus(values):
+        total = values[0].astype(jnp.float32)
+        for value in values[1:]:
+            total = total + value.astype(jnp.float32)
+        return total
+
+    for n, d in enumerate(order):
+        slot = LINE + line(d)
+        arrived(from_b.at[slot], rb_recv.at[slot])
+        contrib[slot] = plus([contrib[slot], from_b[slot]]).astype(jnp.bfloat16)
+        to = line(d)
+        go(remote(contrib.at[slot], from_a.at[to], ra_send.at[n], ra_recv.at[to], near_a))
+    for n, d in enumerate(order):
+        slot = line(d)
+        arrived(from_b.at[slot], rb_recv.at[slot])
+        arrived(from_a.at[slot], ra_recv.at[slot])
+        total = plus([contrib[slot], from_b[slot], from_a[slot]])
+        if d:
+            contrib[slot] = total.astype(jnp.bfloat16)
+            to = LINE - 1 - d
+            chip = base + 4 * slot
+            go(remote(contrib.at[slot], from_z.at[to], rz_send.at[n], rz_recv.at[to], chip))
+        else:
+            contrib[slot] = total.astype(jnp.bfloat16)
+    for d in range(LINE - 1):
+        arrived(from_z.at[d], rz_recv.at[d])
+    out_ref[...] = plus([contrib[z], from_z[0], from_z[1], from_z[2]]).astype(jnp.bfloat16)
+    for copy in pending:
+        copy.wait_send()
+
+    def drain(n, carry):
+        exchange(n // tiles, n % tiles).wait_send()
+        return carry
+
+    lax.fori_loop(0, LINE * tiles, drain, 0)
+
+
+def fused(tokens, routes, route_scores, placement, w_in, w_out):
+    rows, cols = tokens.shape
+    hidden = w_in.shape[3]
+    tiles = hidden // TILE
+    table = expert_weights(routes, route_scores, placement)
+    high = lax.reduce_precision(table, 8, 7)
+    middle = lax.reduce_precision(table - high, 8, 7)
+    low = table - high - middle
+    thirds = [third.astype(jnp.bfloat16) for third in (high, middle, low)]
+    filler = jnp.zeros((rows, LANES - 3 * table.shape[1]), jnp.bfloat16)
+    ext = jnp.concatenate([tokens, *thirds, filler], axis=1)
+    slots = LINE * LINE
+    bf16 = jnp.bfloat16
+    dma = pltpu.SemaphoreType.DMA
+    return pl.pallas_call(
+        layer_kernel,
+        out_shape=jax.ShapeDtypeStruct((rows, cols), bf16),
+        in_specs=[
+            pl.BlockSpec(memory_space=pltpu.VMEM),
+            pl.BlockSpec(memory_space=pl.ANY),
+            pl.BlockSpec(memory_space=pl.ANY),
+        ],
+        out_specs=pl.BlockSpec(memory_space=pltpu.VMEM),
+        scratch_shapes=[
+            pltpu.VMEM((slots, rows, cols + LANES), bf16),
+            pltpu.VMEM((cols, hidden), bf16),
+            pltpu.VMEM((cols, hidden), bf16),
+            pltpu.VMEM((2, cols, 2, LANES), bf16),
+            pltpu.VMEM((hidden, cols), bf16),
+            pltpu.VMEM((slots, rows, cols), bf16),
+            pltpu.VMEM((2 * LINE, rows, cols), bf16),
+            pltpu.VMEM((LINE, rows, cols), bf16),
+            pltpu.VMEM((LINE - 1, rows, cols), bf16),
+            pltpu.VMEM((tiles, 2, LINE * rows, TILE), jnp.float32),
+            pltpu.VMEM((LINE, tiles, 2, LINE * rows, TILE), bf16),
+            pltpu.VMEM((LINE, tiles, 2, LINE * rows, TILE), bf16),
+            pltpu.VMEM((LINE * rows, hidden), bf16),
+            dma((2,)), dma, dma((LINE - 1,)), dma((LINE,)), dma((2 * LINE,)), dma((slots,)),
+            dma((LINE, tiles)), dma((LINE, tiles)),
+            dma((2 * LINE,)), dma((2 * LINE,)), dma((LINE,)), dma((LINE,)),
+            dma((LINE,)), dma((LINE - 1,)),
+        ],
+        compiler_params=pltpu.CompilerParams(
+            collective_id=0, has_side_effects=True, vmem_limit_bytes=67043328
+        ),
+    )(ext, w_in, w_out)
+
+
+def on_device(tokens, routes, route_scores, placement, w_in, w_out):
+    tok_rows = tokens.shape[0]
+    experts = placement.shape[0]
+    fits = experts == 4 * LINE and lax.axis_size("replica") == 2
+    if fits and 2 * tok_rows * routes.shape[1] // experts >= tok_rows:
+        return fused(tokens, routes, route_scores, placement, w_in, w_out)
+    return packed(tokens, routes, route_scores, placement, w_in, w_out)
+
+
 def solution(mesh):
     in_specs = (
         P("expert", "replica"),

time: 455 us -> 200 us (0.44)
  the two profiles are of different devices: /device:TPU:28 before, /device:TPU:0 now
where the time goes in v2:
time: 200 us
  Pallas kernels  194 us (97%)
  local copies, waits for them, and re-layouts  3.87 us (2%)
  other arithmetic  2.22 us (1%)
    pallas_call x1, Pallas kernels, fused(): pl.pallas_call(layer_kernel, out_shape=jax.ShapeDtypeStruct((rows, cols),...  194 us

profile of v2, /device:TPU:0, one launch (start us, length us, event | category | flops | bytes accessed | tf_op | source)
XLA Modules:
  0.0 200.1 jit_solution(11652360799536713081)
XLA Ops:
  0.0 0.7 reduce_sum.28
  0.7 0.7 multiply_divide_fusion
  1.4 0.8 select_reduce_fusion.1
  2.2 0.1 copy.12
  2.3 0.1 copy.11
  2.4 1.9 concatenate.3.ext_ref
  4.3 194.0 %shard_map.64 = bf16[64,3584]{1,0:T(8,128)(2,1)} custom-call(bf16[64,3712]{1,0:T(8,128)(2,1)} %concatenate.3.ext_ref, bf16[1,3584,2,1024]{3,2,1,0:T(2,128)(2,1)} %w_in_ref.1, bf16[1,1024,3584]{2,1,0:T(8,128)(2,1)} %w_out_ref.1), custom_call_target="tpu_custom_call" | custom-call | tf_op jit(solution)/shard_map/pallas_call | solution.py:289
  198.3 1.8 copy.15
  (4 shorter events, 0.0 us)

commit v3 on v2

--- a/solution.py
+++ b/solution.py
@@ -95,7 +95,7 @@
         )
 
     def arrived(ref, recv):
-        remote(ref, ref, a_send.at[0], recv, near_a).wait_recv()
+        remote(ref, ref, a_send.at[0, 0], recv, near_a).wait_recv()
 
     def stage_copy(ct):
         return pltpu.make_async_copy(
@@ -108,10 +108,23 @@
         copy.start()
         pending.append(copy)
 
-    go(remote(ext_ref, xs.at[LINE + z], a_send.at[0], x_recv.at[LINE + z], near_a))
-    go(remote(ext_ref, xs.at[2 * LINE + z], b_send.at[0], x_recv.at[2 * LINE + z], near_b))
-    for d in (1, 3, 2):
-        go(remote(ext_ref, xs.at[z], z_send.at[d - 1], x_recv.at[z], base + 4 * line(d)))
+    part_rows = rows // 2
+
+    def pass_on(source, to, send, chip, h):
+        part = pl.ds(h * part_rows, part_rows)
+        go(remote(source, xs.at[to, part], send.at[h], x_recv.at[to, h], chip))
+
+    def landed(slot, h):
+        part = pl.ds(h * part_rows, part_rows)
+        arrived(xs.at[slot, part], x_recv.at[slot, h])
+        return xs.at[slot, part]
+
+    for h in range(2):
+        own = ext_ref.at[pl.ds(h * part_rows, part_rows)]
+        pass_on(own, LINE + z, a_send.at[0], near_a, h)
+        pass_on(own, 2 * LINE + z, b_send.at[0], near_b, h)
+        for d in (1, 3, 2):
+            pass_on(own, z, z_send.at[d - 1], base + 4 * line(d), h)
     stage_copy(0).start()
     stage_copy(1).start()
     out_weights = pltpu.make_async_copy(w_out_ref.at[0], wo, wo_sem)
@@ -142,16 +155,16 @@
 
     def own_line_on(d, n):
         slot = line(d)
-        arrived(xs.at[slot], x_recv.at[slot])
-        go(remote(xs.at[slot], xs.at[LINE + slot], a_send.at[n], x_recv.at[LINE + slot], near_a))
-        to = 2 * LINE + slot
-        go(remote(xs.at[slot], xs.at[to], b_send.at[n], x_recv.at[to], near_b))
+        for h in range(2):
+            held = landed(slot, h)
+            pass_on(held, LINE + slot, a_send.at[n], near_a, h)
+            pass_on(held, 2 * LINE + slot, b_send.at[n], near_b, h)
 
     def a_line_on(d, n):
         slot = LINE + line(d)
-        arrived(xs.at[slot], x_recv.at[slot])
-        to = 2 * LINE + slot
-        go(remote(xs.at[slot], xs.at[to], b_send.at[LINE + n], x_recv.at[to], near_b))
+        for h in range(2):
+            held = landed(slot, h)
+            pass_on(held, 2 * LINE + slot, b_send.at[LINE + n], near_b, h)
 
     all_tiles = list(range(hidden // LANES))
     quarter = max(1, len(all_tiles) // 4)
@@ -176,7 +189,7 @@
     def exchange(s, j):
         return remote(sent.at[s, j], got.at[s, j], p_send.at[s, j], p_recv.at[s, j], me, 1 - core)
 
-    def step(s, group):
+    def step(s, group, ship=None):
         block = pl.ds(group * LINE, LINE)
 
         def first(j, carry):
@@ -209,31 +222,40 @@
         def third(j, carry):
             at = pl.ds(pl.multiple_of(j * TILE, TILE), TILE)
             value = jnp.dot(act[...], wo[:, at], preferred_element_type=jnp.float32)
-            value = value.astype(jnp.bfloat16).astype(jnp.float32) * scale
+            value = value * scale
             contrib[block, :, at] = value.astype(jnp.bfloat16).reshape(LINE, rows, TILE)
             return carry
 
-        lax.fori_loop(0, cols // TILE, third, 0)
+        out_tiles = wide // TILE
+        for h in range(2):
+            lax.fori_loop(h * out_tiles, (h + 1) * out_tiles, third, 0)
+            if ship is not None:
+                ship(h)
+
+    wide = cols // 2
+    order = (1, 3, 2, 0)
+
+    def cut(h):
+        return slice(h * wide, (h + 1) * wide)
+
+    def ship_b(from_line, to_line, h):
+        for n, d in enumerate(order):
+            src, to = from_line * LINE + line(d), to_line * LINE + line(d)
+            go(remote(contrib.at[src, :, cut(h)], from_b.at[to, :, cut(h)],
+                      rb_send.at[to_line * LINE + n, h], rb_recv.at[to, h], near_b))
 
     step(0, 0)
     for d in range(LINE):
-        slot = 2 * LINE + line(d)
-        arrived(xs.at[slot], x_recv.at[slot])
+        for h in range(2):
+            landed(2 * LINE + line(d), h)
     step(1, 1 + core)
     step(2, 2 - core)
-    order = (1, 3, 2, 0)
-    for n, d in enumerate(order):
-        src = 2 * LINE + line(d)
-        to = line(d)
-        go(remote(contrib.at[src], from_b.at[to], rb_send.at[n], rb_recv.at[to], near_b))
+    for h in range(2):
+        ship_b(2, 0, h)
     for d in range(LINE):
-        slot = 3 * LINE + line(d)
-        arrived(xs.at[slot], x_recv.at[slot])
-    step(3, 3)
-    for n, d in enumerate(order):
-        src = 3 * LINE + line(d)
-        to = LINE + line(d)
-        go(remote(contrib.at[src], from_b.at[to], rb_send.at[LINE + n], rb_recv.at[to], near_b))
+        for h in range(2):
+            landed(3 * LINE + line(d), h)
+    step(3, 3, lambda h: ship_b(3, 1, h))
 
     def plus(values):
         total = values[0].astype(jnp.float32)
@@ -241,27 +263,40 @@
             total = total + value.astype(jnp.float32)
         return total
 
+    def to_a(h, n, d):
+        slot, to = LINE + line(d), line(d)
+        arrived(from_b.at[slot, :, cut(h)], rb_recv.at[slot, h])
+        contrib[slot, :, cut(h)] = plus(
+            [contrib[slot, :, cut(h)], from_b[slot, :, cut(h)]]
+        ).astype(jnp.bfloat16)
+        go(remote(contrib.at[slot, :, cut(h)], from_a.at[to, :, cut(h)],
+                  ra_send.at[n, h], ra_recv.at[to, h], near_a))
+
+    def to_z(h, n, d):
+        slot = line(d)
+        arrived(from_b.at[slot, :, cut(h)], rb_recv.at[slot, h])
+        arrived(from_a.at[slot, :, cut(h)], ra_recv.at[slot, h])
+        contrib[slot, :, cut(h)] = plus(
+            [contrib[slot, :, cut(h)], from_b[slot, :, cut(h)], from_a[slot, :, cut(h)]]
+        ).astype(jnp.bfloat16)
+        if d:
+            to = LINE - 1 - d
+            go(remote(contrib.at[slot, :, cut(h)], from_z.at[to, :, cut(h)],
+                      rz_send.at[n, h], rz_recv.at[to, h], base + 4 * slot))
+
     for n, d in enumerate(order):
-        slot = LINE + line(d)
-        arrived(from_b.at[slot], rb_recv.at[slot])
-        contrib[slot] = plus([contrib[slot], from_b[slot]]).astype(jnp.bfloat16)
-        to = line(d)
-        go(remote(contrib.at[slot], from_a.at[to], ra_send.at[n], ra_recv.at[to], near_a))
+        to_a(0, n, d)
     for n, d in enumerate(order):
-        slot = line(d)
-        arrived(from_b.at[slot], rb_recv.at[slot])
-        arrived(from_a.at[slot], ra_recv.at[slot])
-        total = plus([contrib[slot], from_b[slot], from_a[slot]])
-        if d:
-            contrib[slot] = total.astype(jnp.bfloat16)
-            to = LINE - 1 - d
-            chip = base + 4 * slot
-            go(remote(contrib.at[slot], from_z.at[to], rz_send.at[n], rz_recv.at[to], chip))
-        else:
-            contrib[slot] = total.astype(jnp.bfloat16)
-    for d in range(LINE - 1):
-        arrived(from_z.at[d], rz_recv.at[d])
-    out_ref[...] = plus([contrib[z], from_z[0], from_z[1], from_z[2]]).astype(jnp.bfloat16)
+        to_a(1, n, d)
+        to_z(0, n, d)
+    for n, d in enumerate(order):
+        to_z(1, n, d)
+    for h in range(2):
+        for d in range(LINE - 1):
+            arrived(from_z.at[d, :, cut(h)], rz_recv.at[d, h])
+        out_ref[:, cut(h)] = plus(
+            [contrib[z, :, cut(h)]] + [from_z[d, :, cut(h)] for d in range(LINE - 1)]
+        ).astype(jnp.bfloat16)
     for copy in pending:
         copy.wait_send()
 
@@ -309,10 +344,10 @@
             pltpu.VMEM((LINE, tiles, 2, LINE * rows, TILE), bf16),
             pltpu.VMEM((LINE, tiles, 2, LINE * rows, TILE), bf16),
             pltpu.VMEM((LINE * rows, hidden), bf16),
-            dma((2,)), dma, dma((LINE - 1,)), dma((LINE,)), dma((2 * LINE,)), dma((slots,)),
+            dma((2,)), dma, dma((LINE - 1, 2)), dma((LINE, 2)), dma((2 * LINE, 2)), dma((slots, 2)),
             dma((LINE, tiles)), dma((LINE, tiles)),
-            dma((2 * LINE,)), dma((2 * LINE,)), dma((LINE,)), dma((LINE,)),
-            dma((LINE,)), dma((LINE - 1,)),
+            dma((2 * LINE, 2)), dma((2 * LINE, 2)), dma((LINE, 2)), dma((LINE, 2)),
+            dma((LINE, 2)), dma((LINE - 1, 2)),
         ],
         compiler_params=pltpu.CompilerParams(
             collective_id=0, has_side_effects=True, vmem_limit_bytes=67043328

time: 200 us -> 194 us (0.970)
  Pallas kernels: 194 us -> 187 us
    pallas_call x1, Pallas kernels: 194 us -> 187 us  [fused(): pl.pallas_call(layer_kernel, out_shape=jax.ShapeDtypeStruct((rows, cols),...]
where the time goes in v3:
time: 194 us; the launch traced here: 193 us
  Pallas kernels  187 us (96%)
  local copies, waits for them, and re-layouts  3.87 us (2%)
  other arithmetic  2.22 us (1%)
    pallas_call x1, Pallas kernels, fused(): pl.pallas_call(layer_kernel, out_shape=jax.ShapeDtypeStruct((rows, cols),...  187 us

profile of v3, /device:TPU:0, one launch (start us, length us, event | category | flops | bytes accessed | tf_op | source)
XLA Modules:
  0.0 193.3 jit_solution(8599562670869001218)
XLA Ops:
  0.0 0.7 reduce_sum.28
  0.7 0.7 multiply_divide_fusion
  1.4 0.8 select_reduce_fusion.1
  2.2 0.1 copy.12
  2.3 0.1 copy.11
  2.4 1.9 concatenate.3.ext_ref
  4.3 187.1 %shard_map.64 = bf16[64,3584]{1,0:T(8,128)(2,1)} custom-call(bf16[64,3712]{1,0:T(8,128)(2,1)} %concatenate.3.ext_ref, bf16[1,3584,2,1024]{3,2,1,0:T(2,128)(2,1)} %w_in_ref.1, bf16[1,1024,3584]{2,1,0:T(8,128)(2,1)} %w_out_ref.1), custom_call_target="tpu_custom_call" | custom-call | tf_op jit(solution)/shard_map/pallas_call | solution.py:324
  191.4 1.8 copy.15
  (4 shorter events, 0.0 us)
